TPU v7x, 32 devices: a whole 2x2x4 slice. The times are simulated.
32 devices in a mesh: dp: 4 (over z), ctx: 8 (over y, x, core).
Axes of the slice: x: 2, y: 2, z: 4, core: 2. Of those that a mesh axis runs over, the one named last changes fastest.
Arguments:
- queries: bfloat16 [4, 4096, 1024], P('dp', 'ctx'), may hold values from -6 to 6
- key_vectors: bfloat16 [4, 4096, 1024], P('dp', 'ctx'), may hold values from -6 to 6
- value_vectors: bfloat16 [4, 4096, 1024], P('dp', 'ctx'), may hold values from -6 to 6
- out_grad: bfloat16 [4, 4096, 1024], P('dp', 'ctx'), may hold values from -6 to 6
- column_bias: float32 [8], replicated, may hold values from -1 to 2
- column_offsets: int32 [1], replicated, may hold values from 0 to 63
Outputs:
- attended: bfloat16 [4, 4096, 1024], P('dp', 'ctx')
- query_grad: bfloat16 [4, 4096, 1024], P('dp', 'ctx')
- key_grad: bfloat16 [4, 4096, 1024], P('dp', 'ctx')
- value_grad: bfloat16 [4, 4096, 1024], P('dp', 'ctx')
- bias_grad: float32 [8], replicated
All inputs are finite; a program needn't handle non-finite values.
Results may differ from a plain program's by a relative error of at most 0.005.
The roundings to bfloat16 on the way count: a program that leaves them out, or rounds other values in their place, can miss the bound.
Values may be sent and summed in bfloat16 or wider, within the bound.
A program may use at most 128 MiB of HBM per device.

v0:
```python
import jax
import jax.numpy as jnp
from jax import lax
from jax.sharding import PartitionSpec as P

HEADS = 8
HEAD_DIM = 128
LOCAL_BAND = 512
STRIDE = 4096
CB = 64
TOKENS_PER_SHARD = 512


def from_behind(value, axis, by):
    size = lax.axis_size(axis)
    pairs = [(i, i + by) for i in range(size) if 0 <= i + by < size]
    return lax.ppermute(value, axis, pairs)


def column_flags(positions, offsets):
    window = positions // STRIDE
    within = positions % STRIDE
    picks = window[:, None] == jnp.arange(offsets.shape[0], dtype=jnp.int32)[None, :]
    offset_at = jnp.sum(jnp.where(picks, offsets[None, :], 0), axis=1)
    return (positions >= 0) & (within // CB == offset_at)


def head_block(qh, kb, vb, kc, vc, doh, bias_h, band_ok, band_col, col_ok):
    scale = HEAD_DIM ** (-0.5)
    sb = (
        jnp.dot(qh, kb.T, preferred_element_type=jnp.float32) * scale
        + jnp.where(band_col, bias_h, 0.0)[None, :]
    )
    sc = jnp.dot(qh, kc.T, preferred_element_type=jnp.float32) * scale + bias_h
    sb = jnp.where(band_ok, sb, -jnp.inf)
    sc = jnp.where(col_ok, sc, -jnp.inf)
    top = jnp.maximum(jnp.max(sb, axis=1), jnp.max(sc, axis=1))
    pb = jnp.exp(sb - top[:, None])
    pc = jnp.exp(sc - top[:, None])
    total = jnp.sum(pb, axis=1) + jnp.sum(pc, axis=1)
    wb = pb / total[:, None]
    wc = pc / total[:, None]
    wb16 = wb.astype(jnp.bfloat16)
    wc16 = wc.astype(jnp.bfloat16)
    mixed = jnp.dot(wb16, vb, preferred_element_type=jnp.float32) + jnp.dot(
        wc16, vc, preferred_element_type=jnp.float32
    )
    oh = mixed.astype(jnp.bfloat16)
    delta = jnp.sum(doh.astype(jnp.float32) * oh.astype(jnp.float32), axis=1)
    dsb = wb * (jnp.dot(doh, vb.T, preferred_element_type=jnp.float32) - delta[:, None])
    dsc = wc * (jnp.dot(doh, vc.T, preferred_element_type=jnp.float32) - delta[:, None])
    dbias = jnp.sum(jnp.where(band_col[None, :], dsb, 0.0)) + jnp.sum(dsc)
    dsb16 = dsb.astype(jnp.bfloat16)
    dsc16 = dsc.astype(jnp.bfloat16)
    dq = (
        (
            jnp.dot(dsb16, kb, preferred_element_type=jnp.float32)
            + jnp.dot(dsc16, kc, preferred_element_type=jnp.float32)
        )
        * scale
    ).astype(jnp.bfloat16)
    dkb = jnp.dot(dsb16.T, qh, preferred_element_type=jnp.float32) * scale
    dvb = jnp.dot(wb16.T, doh, preferred_element_type=jnp.float32)
    dkc = jnp.dot(dsc16.T, qh, preferred_element_type=jnp.float32) * scale
    dvc = jnp.dot(wc16.T, doh, preferred_element_type=jnp.float32)
    return (oh, dq, dkb, dvb, dkc, dvc, dbias, top, total, delta)


def separate_heads(x):
    return x.reshape(x.shape[0], HEADS, HEAD_DIM).transpose(1, 0, 2)


def join_heads(x):
    return x.transpose(1, 0, 2).reshape(x.shape[1], HEADS * HEAD_DIM)


def per_device(queries, key_vectors, value_vectors, out_grad, column_bias, column_offsets):
    here = lax.axis_index("ctx")
    count = lax.axis_size("ctx")
    start_position = here * TOKENS_PER_SHARD
    width = queries.shape[2]
    query_rows = queries[0]
    key_rows = key_vectors[0]
    value_rows = value_vectors[0]
    grad_rows = out_grad[0]
    ncol = column_offsets.shape[0]
    block_starts = jnp.arange(ncol, dtype=jnp.int32) * STRIDE + column_offsets * CB
    colpos = jnp.repeat(block_starts, CB) + jnp.tile(jnp.arange(CB, dtype=jnp.int32), ncol)
    window = start_position // STRIDE
    own_start = window * STRIDE + column_offsets[window] * CB
    local = jnp.clip(own_start - start_position, 0, TOKENS_PER_SHARD - CB)
    piece_k = lax.dynamic_slice_in_dim(key_rows, local, CB, 0)
    piece_v = lax.dynamic_slice_in_dim(value_rows, local, CB, 0)
    pieces_k, pieces_v = (
        lax.all_gather(piece_k, "ctx", axis=0, tiled=True),
        lax.all_gather(piece_v, "ctx", axis=0, tiled=True),
    )
    owner = block_starts // TOKENS_PER_SHARD
    col_k = pieces_k.reshape(count, CB, width)[owner].reshape(ncol * CB, width)
    col_v = pieces_v.reshape(count, CB, width)[owner].reshape(ncol * CB, width)
    prev_k, prev_v = from_behind((key_rows, value_rows), "ctx", 1)
    band_k = jnp.concatenate([prev_k, key_rows], axis=0)
    band_v = jnp.concatenate([prev_v, value_rows], axis=0)
    qpos = start_position + jnp.arange(TOKENS_PER_SHARD, dtype=jnp.int32)
    kpos = start_position - LOCAL_BAND + jnp.arange(LOCAL_BAND + TOKENS_PER_SHARD, dtype=jnp.int32)
    gap = qpos[:, None] - kpos[None, :]
    band_ok = (kpos[None, :] >= 0) & (gap >= 0) & (gap < LOCAL_BAND)
    band_col = column_flags(kpos, column_offsets)
    col_ok = colpos[None, :] <= qpos[:, None] - LOCAL_BAND

    def per_head(items):
        return head_block(
            items[0],
            items[1],
            items[2],
            items[3],
            items[4],
            items[5],
            items[6],
            band_ok,
            band_col,
            col_ok,
        )

    results = lax.map(
        per_head,
        (
            separate_heads(query_rows),
            separate_heads(band_k),
            separate_heads(band_v),
            separate_heads(col_k),
            separate_heads(col_v),
            separate_heads(grad_rows),
            column_bias,
        ),
    )
    oh, dq, dkb, dvb, dkc, dvc, dbias, top, total, delta = results
    attended = join_heads(oh)
    query_grad = join_heads(dq)
    dk_band = join_heads(dkb)
    dv_band = join_heads(dvb)
    own_dk = dk_band[dk_band.shape[0] - TOKENS_PER_SHARD :]
    own_dv = dv_band[dv_band.shape[0] - TOKENS_PER_SHARD :]
    back_k, back_v = from_behind((dk_band[:LOCAL_BAND], dv_band[:LOCAL_BAND]), "ctx", -1)
    own_dk = own_dk.at[TOKENS_PER_SHARD - LOCAL_BAND :].add(back_k)
    own_dv = own_dv.at[TOKENS_PER_SHARD - LOCAL_BAND :].add(back_v)
    summed_k, summed_v = lax.psum((join_heads(dkc), join_heads(dvc)), "ctx")
    flags = column_flags(qpos, column_offsets)
    source = jnp.clip(qpos // STRIDE * CB + qpos % CB, 0, ncol * CB - 1)
    own_dk = own_dk + jnp.where(flags[:, None], summed_k[source], 0.0)
    own_dv = own_dv + jnp.where(flags[:, None], summed_v[source], 0.0)
    bias_grad = lax.psum(dbias, ("dp", "ctx"))
    return (
        attended[None],
        query_grad[None],
        own_dk.astype(jnp.bfloat16)[None],
        own_dv.astype(jnp.bfloat16)[None],
        bias_grad,
    )


def solution(mesh):
    placed = (
        P("dp", "ctx", None),
        P("dp", "ctx", None),
        P("dp", "ctx", None),
        P("dp", "ctx", None),
        P(),
        P(),
    )
    return jax.shard_map(
        per_device,
        mesh=mesh,
        in_specs=placed,
        out_specs=(
            P("dp", "ctx", None),
            P("dp", "ctx", None),
            P("dp", "ctx", None),
            P("dp", "ctx", None),
            P(),
        ),
        check_vma=False,
    )
```

profile of v0, /device:TPU:0, one launch (start us, length us, event | category | flops | bytes accessed | tf_op | source)
XLA Modules:
  0.0 354.4 jit_solution(14615889557479074196)
XLA Ops:
  8.0 1.6 constant_dynamic-slice_fusion
  9.6 1.6 constant_dynamic-slice_fusion.1
  11.3 1.5 copy.22
  12.8 3.3 collective-permute-start
  16.7 4.5 %collective-permute-start.1 = (bf16[512,1024]{0,1:T(8,128)(2,1)S(1)}, bf16[512,1024]{0,1:T(8,128)(2,1)}, u32[]{:S(2)}, u32[]{:S(2)}) collective-permute-start(bf16[512,1024]{0,1:T(8,128)(2,1)S(1)} %bitcast.242), channel_id=1, source_target_pairs={{0,1},{1,2},{2,3},{3,4},{4,5},{5,6},{6,7},{8,9},{9,10},{10,11},{11... | collective-permute-start | bytes 3145736 | tf_op jit(solution)/shard_map/ppermute | solution.py:17
  22.7 2.3 copy.26
  25.1 2.9 maximum_bitcast_fusion
  28.0 2.9 maximum_bitcast_fusion.1
  30.9 7.3 %all-gather.7.cloned.1.call-done = bf16[1,512,1024]{2,1,0:T(8,128)(2,1)} async-done(((bf16[1,64,1024]{2,1,0:T(8,128)(2,1)}), bf16[1,512,1024]{2,1,0:T(8,128)(2,1)}) %all-gather.7.cloned.1.call-update) | async-done | bytes 1048592 | tf_op jit(solution)/shard_map/all_gather | solution.py:96
  38.2 25.5 %all-gather.5.cloned.1.call-done = bf16[1,512,1024]{2,1,0:T(8,128)(2,1)} async-done(((bf16[1,64,1024]{2,1,0:T(8,128)(2,1)}), bf16[1,512,1024]{2,1,0:T(8,128)(2,1)}) %all-gather.5.cloned.1.call-update) | async-done | bytes 1048592 | tf_op jit(solution)/shard_map/all_gather | solution.py:95
  65.4 169.8 %while.29 = (s32[]{:T(128)}, bf16[8,512,128]{1,2,0:T(8,128)(2,1)}, bf16[8,512,128]{2,1,0:T(8,128)(2,1)}, f32[8,1024,128]{2,1,0:T(8,128)}, f32[8,1024,128]{2,1,0:...) while((s32[]{:T(128)}, bf16[8,512,128]{1,2,0:T(8,128)(2,1)}, ...), condition=%wide.region_8.9_spmd.clone, body=%wide.region_0.8_spmd.clone.sunk | while | flops 869654016 | bytes 19551504 | solution.py:125
  67.3 2.0 fusion.160
  70.7 1.6 fusion.170
  72.3 1.6 fusion.164
  73.9 1.6 bitcast_dynamic-update-slice_fusion.2
  77.8 2.5 select_reduce_fusion.2
  88.6 2.0 fusion.160
  91.9 1.6 fusion.170
  93.5 1.6 fusion.164
  95.1 1.6 bitcast_dynamic-update-slice_fusion.2
  96.8 1.5 fusion.167
  99.0 2.5 select_reduce_fusion.2
  109.8 2.0 fusion.160
  113.2 1.6 fusion.170
  114.8 1.6 fusion.164
  116.4 1.6 bitcast_dynamic-update-slice_fusion.2
  118.1 1.5 fusion.167
  120.2 2.5 select_reduce_fusion.2
  131.0 2.0 fusion.160
  134.4 1.6 fusion.170
  136.0 1.6 fusion.164
  137.6 1.6 bitcast_dynamic-update-slice_fusion.2
  139.3 1.5 fusion.167
  141.4 2.5 select_reduce_fusion.2
  152.2 2.0 fusion.160
  155.6 1.6 fusion.170
  157.2 1.6 fusion.164
  158.8 1.6 bitcast_dynamic-update-slice_fusion.2
  162.7 2.5 select_reduce_fusion.2
  173.5 2.0 fusion.160
  176.8 1.6 fusion.170
  178.4 1.6 fusion.164
  180.1 1.6 bitcast_dynamic-update-slice_fusion.2
  183.9 2.5 select_reduce_fusion.2
  194.7 2.0 fusion.160
  198.1 1.6 fusion.170
  199.6 1.6 fusion.164
  201.3 1.6 bitcast_dynamic-update-slice_fusion.2
  202.9 1.5 fusion.167
  205.1 2.5 select_reduce_fusion.2
  215.9 2.0 fusion.160
  219.3 1.6 fusion.170
  220.9 1.6 fusion.164
  222.5 1.6 bitcast_dynamic-update-slice_fusion.2
  226.4 2.5 select_reduce_fusion.2
  235.3 4.0 %slice_bitcast_fusion.3 = (f32[8,64,8,128]{3,2,1,0:T(8,128)}, f32[8,64,8,128]{3,2,1,0:T(8,128)S(1)}) fusion(f32[1024,8,128]{2,0,1:T(8,128)} %bitcast.240), kind=kLoop, calls=%fused_computation.130 | loop fusion | bytes 8388608
  239.2 1.6 copy.64
  242.3 1.6 slice_bitcast_fusion.1
  243.9 1.6 copy.63
  248.4 79.4 %psum.23 = f32[8]{0:T(128)} all-reduce(f32[8]{0:T(128)S(1)} %get-tuple-element.149), channel_id=1, replica_groups=mesh['dp'=4,'ctx'=8] {'dp','ctx'}, use_global_device_ids=true, to_apply=%region_11.12 | all-reduce | flops 8 | bytes 64 | tf_op jit(solution)/shard_map/psum | solution.py:152
  331.1 4.3 %all-reduce.3.cloned.1.call-done = (f32[64,1024]{1,0:T(8,128)}, f32[64,1024]{1,0:T(8,128)}) async-done(((f32[64,1024]{1,0:T(8,128)}, f32[64,1024]{1,0:T(8,128)}), (f32[64,1024]{1,0:T(8,128)}, f32[64,1024]{1,0:T(8,128)})) %all-reduce.3.cloned.1.call-update) | async-done | bytes 524304 | tf_op jit(solution)/shard_map/psum | solution.py:147
  335.3 3.8 %gather_fusion = f32[512,1024]{1,0:T(8,128)S(1)} fusion(f32[64,1024]{1,0:T(8,128)} %get-tuple-element.315, s32[1024]{0:T(1024)S(1)} %pad_clamp_fusion), kind=kCustom, calls=%fused_computation | custom fusion | bytes 4196352 | tf_op jit(solution)/shard_map/gather | solution.py:150
  339.2 2.7 gather_fusion.1
  341.8 6.0 %fusion.99 = (bf16[1,512,1024]{2,1,0:T(8,128)(2,1)}, bf16[1,512,1024]{2,1,0:T(8,128)(2,1)}) fusion(f32[512,1024]{1,0:T(8,128)} %gather_fusion.1, f32[512,1024]{1,0:T(8,128)} %collective-permute-done.3, f32[8,64,8,128]{3,2,1,0:T(8,128)} %get-tuple-element.327, pred[512]{0:T(512)(128)(4,1)S(1)} %fusion.108, f32[512,1024]{1,0:T(8,128)S(1)} %gather_fusion, ...), kind=kLoop, calls=%fused_computation.134 | loop fusion | flops 4194304 | bytes 14680576 | tf_op jit(solution)/shard_map/convert_element_type | solution.py:157
  (180 shorter events, 91.2 us)
Async XLA Ops:
  7.2 9.0 %copy-start.3 = (bf16[1,512,1024]{2,1,0:T(8,128)(2,1)S(1)}, bf16[1,512,1024]{2,1,0:T(8,128)(2,1)}, u32[]{:S(2)}) copy-start(bf16[1,512,1024]{2,1,0:T(8,128)(2,1)} %param.18) | copy-start | bytes 3145732
  7.2 31.1 %all-gather.7.cloned.1.call-start = ((), (), s32[]{:S(2)}) async-start(), calls=%async_computation.1 | async-start | bytes 1179648 | tf_op jit(solution)/shard_map/all_gather | solution.py:96
  9.6 54.1 %all-gather.5.cloned.1.call-start = ((), (), s32[]{:S(2)}) async-start(), calls=%async_computation | async-start | bytes 1179648 | tf_op jit(solution)/shard_map/all_gather | solution.py:95
  11.2 324.1 %all-reduce.3.cloned.1.call-start = ((), (), s32[]{:S(2)}) async-start(), calls=%async_computation.2 | async-start | bytes 1048576 | tf_op jit(solution)/shard_map/psum | solution.py:147
  12.8 12.3 %collective-permute-start = (bf16[512,1024]{0,1:T(8,128)(2,1)S(1)}, bf16[512,1024]{0,1:T(8,128)(2,1)}, u32[]{:S(2)}, u32[]{:S(2)}) collective-permute-start(bf16[512,1024]{0,1:T(8,128)(2,1)S(1)} %bitcast.244), channel_id=1, source_target_pairs={{0,1},{1,2},{2,3},{3,4},{4,5},{5,6},{6,7},{8,9},{9,10},{10,11},{11... | collective-permute-start | bytes 3145736 | tf_op jit(solution)/shard_map/ppermute | solution.py:17
  16.7 11.3 %collective-permute-start.1 = (bf16[512,1024]{0,1:T(8,128)(2,1)S(1)}, bf16[512,1024]{0,1:T(8,128)(2,1)}, u32[]{:S(2)}, u32[]{:S(2)}) collective-permute-start(bf16[512,1024]{0,1:T(8,128)(2,1)S(1)} %bitcast.242), channel_id=1, source_target_pairs={{0,1},{1,2},{2,3},{3,4},{4,5},{5,6},{6,7},{8,9},{9,10},{10,11},{11... | collective-permute-start | bytes 3145736 | tf_op jit(solution)/shard_map/ppermute | solution.py:17
  28.0 37.5 %copy-start.2 = (bf16[1,512,1024]{1,2,0:T(8,128)(2,1)S(1)}, bf16[1,512,1024]{1,2,0:T(8,128)(2,1)}, u32[]{:S(2)}) copy-start(bf16[1,512,1024]{1,2,0:T(8,128)(2,1)} %copy.26) | copy-start | bytes 3145732
  28.0 37.5 %copy-start.8 = (f32[8]{0:T(128)S(1)}, f32[8]{0:T(128)}, u32[]{:S(2)}) copy-start(f32[8]{0:T(128)} %param.20) | copy-start | bytes 100
  239.2 3.0 copy-start.1
  240.8 101.0 %collective-permute-start.2 = (f32[512,1024]{1,0:T(8,128)}, f32[512,1024]{1,0:T(8,128)}, u32[]{:S(2)}, u32[]{:S(2)}) collective-permute-start(f32[512,1024]{1,0:T(8,128)} %bitcast.178), channel_id=1, source_target_pairs={{1,0},{2,1},{3,2},{4,3},{5,4},{6,5},{7,6},{9,8},{10,9},{11,10},{12... | collective-permute-start | bytes 6291464 | tf_op jit(solution)/shard_map/ppermute | solution.py:17
  243.9 2.9 copy-start.7
  243.9 3.7 %copy-start.6 = (f32[8,64,128]{2,1,0:T(8,128)S(1)}, f32[8,64,128]{2,1,0:T(8,128)}, u32[]{:S(2)}) copy-start(f32[8,64,128]{2,1,0:T(8,128)} %get-tuple-element.146) | copy-start | bytes 786436
  243.9 83.9 %copy-start.5 = (bf16[8,512,128]{2,1,0:T(8,128)(2,1)S(1)}, bf16[8,512,128]{2,1,0:T(8,128)(2,1)}, u32[]{:S(2)}) copy-start(bf16[8,512,128]{2,1,0:T(8,128)(2,1)} %get-tuple-element.144) | copy-start | bytes 3145732
  245.5 96.3 %collective-permute-start.3 = (f32[512,1024]{1,0:T(8,128)}, f32[512,1024]{1,0:T(8,128)}, u32[]{:S(2)}, u32[]{:S(2)}) collective-permute-start(f32[512,1024]{1,0:T(8,128)} %bitcast.177), channel_id=1, source_target_pairs={{1,0},{2,1},{3,2},{4,3},{5,4},{6,5},{7,6},{9,8},{10,9},{11,10},{12... | collective-permute-start | bytes 6291464 | tf_op jit(solution)/shard_map/ppermute | solution.py:17
  327.8 2.0 copy-start.4
  335.3 3.8 %copy-start = (f32[64,1024]{1,0:T(8,128)S(1)}, f32[64,1024]{1,0:T(8,128)}, u32[]{:S(2)}) copy-start(f32[64,1024]{1,0:T(8,128)} %get-tuple-element.316) | copy-start | bytes 786436
Sparse Core Ops, SparseCore 0:
  9.9 28.2 all-gather.6
  40.1 23.5 all-gather.4
  248.4 86.8 all-reduce.2
where the time goes:
time: 357 us; the launch traced here: 354 us
  matrix products  133 us (37%)
  blocking collectives  79.4 us (22%)
  waiting for transfers between devices  37.1 us (10%)
  local copies, waits for them, and re-layouts  36.4 us (10%)
  other arithmetic  32.7 us (9%)
  between operations  14.7 us (4%)
  starting transfers between devices  10.7 us (3%)
  loops' own time  10 us (3%)
    psum x1, blocking collectives, per_device(): bias_grad = lax.psum(dbias, ('dp', 'ctx'))  79.4 us
    all_gather x1, waiting for transfers between devices, per_device(): lax.all_gather(piece_k, 'ctx', axis=0, tiled=True)  25.5 us
    dot_general x8, matrix products, head_block(): jnp.dot(doh, vb.T, preferred_element_type=jnp.float32) - delta[:, None]  19.7 us
    dot_general x8, matrix products, head_block(): jnp.dot(qh, kb.T, preferred_element_type=jnp.float32) * scale  15.9 us
    unnamed x29, local copies, waits for them, and re-layouts  13.2 us
    dot_general x8, matrix products, head_block(): jnp.dot(wb16, vb, preferred_element_type=jnp.float32)  12.9 us
    dot_general x8, matrix products, head_block(): jnp.dot(wc16, vc, preferred_element_type=jnp.float32)  12.9 us
    dot_general x8, matrix products, head_block(): dvb = jnp.dot(wb16.T, doh, preferred_element_type=jnp.float32)  12.7 us
  transfers between devices with their start and end apart: 7, of which 3 were waited for; matrix products, arithmetic and copies ran while one was open for 8% of the time, Pallas kernels for 0%

commit v1 on v0

--- a/solution.py
+++ b/solution.py
@@ -1,6 +1,10 @@
+import functools
+
 import jax
 import jax.numpy as jnp
 from jax import lax
+from jax.experimental import pallas as pl
+from jax.experimental.pallas import tpu as pltpu
 from jax.sharding import PartitionSpec as P
 
 HEADS = 8
@@ -74,7 +78,7 @@
     return x.transpose(1, 0, 2).reshape(x.shape[1], HEADS * HEAD_DIM)
 
 
-def per_device(queries, key_vectors, value_vectors, out_grad, column_bias, column_offsets):
+def per_device_many_windows(queries, key_vectors, value_vectors, out_grad, column_bias, column_offsets):
     here = lax.axis_index("ctx")
     count = lax.axis_size("ctx")
     start_position = here * TOKENS_PER_SHARD
@@ -159,6 +163,395 @@
     )
 
 
+LOG2E = 1.4426950408889634
+SCALE = HEAD_DIM ** (-0.5)
+NEG = -1e30
+HALF = 256
+T = TOKENS_PER_SHARD
+D = HEAD_DIM
+MESH = pl.DeviceIdType.MESH
+NT = (((1,), (1,)), ((), ()))
+TN = (((0,), (0,)), ((), ()))
+
+
+def dot_nt(a, b):
+    return lax.dot_general(a, b, NT, preferred_element_type=jnp.float32)
+
+
+def dot_tn(a, b):
+    return lax.dot_general(a, b, TN, preferred_element_type=jnp.float32)
+
+
+def dot_nn(a, b):
+    return jnp.dot(a, b, preferred_element_type=jnp.float32)
+
+
+def flip(index, step):
+    return index + step * (1 - 2 * ((index // step) % 2))
+
+
+def fold(x):
+    return x[:, :128] + x[:, 128:]
+
+
+def fused_kernel(
+    n,
+    ndp,
+    offs_ref,
+    bias_ref,
+    q_ref,
+    k_ref,
+    v_ref,
+    g_ref,
+    o_ref,
+    dq_ref,
+    dk_ref,
+    dv_ref,
+    db_ref,
+    prev,
+    back,
+    out,
+    own,
+    col,
+    colr,
+    acc,
+    accr,
+    bacc,
+    baccr,
+    flag,
+    masks,
+    halo_s,
+    halo_r,
+    ret_s,
+    ret_r,
+    cg_s,
+    cg_r,
+    red_s,
+    red_r,
+    b_s,
+    b_r,
+):
+    me = lax.axis_index("ctx")
+    mine = lax.axis_index("dp")
+    steps = []
+    while 2 ** len(steps) < n:
+        steps.append(2 ** len(steps))
+    dsteps = []
+    while 2 ** len(dsteps) < ndp:
+        dsteps.append(2 ** len(dsteps))
+    S = len(steps)
+    start = me * T
+    col_row = offs_ref[0:1, :]
+    col_start = col_row[:, 0:128]
+    col_start2 = col_row[:, 0:HALF]
+
+    other = me + 2 * (me % 2) - 1
+    has_other = (other >= 0) & (other < n)
+    barrier = pltpu.get_barrier_semaphore()
+    for st in steps:
+        pl.semaphore_signal(barrier, inc=1, device_id={"ctx": flip(me, st)}, device_id_type=MESH)
+    for st in dsteps:
+        pl.semaphore_signal(barrier, inc=1, device_id={"dp": flip(mine, st)}, device_id_type=MESH)
+
+    @pl.when(has_other)
+    def _():
+        pl.semaphore_signal(barrier, inc=1, device_id={"ctx": other}, device_id_type=MESH)
+
+    for i, ref in ((0, k_ref), (1, v_ref)):
+        block = jnp.zeros((CB, ref.shape[1]), jnp.float32)
+        for r in range(T // CB):
+            held = (col_row == start + r * CB).astype(jnp.float32)
+            block = block + ref[r * CB : (r + 1) * CB, :].astype(jnp.float32) * held
+        col[i * CB : (i + 1) * CB, :] = block.astype(jnp.bfloat16)
+
+    row = lax.broadcasted_iota(jnp.int32, (HALF, HALF), 0)
+    lane = lax.broadcasted_iota(jnp.int32, (HALF, HALF), 1)
+    masks[0] = jnp.where(row > lane, 0.0, NEG)
+    masks[1] = jnp.where(row <= lane, 0.0, NEG)
+    kpos = start - T + lax.broadcasted_iota(jnp.int32, (2 * T, 128), 0)
+    flag[...] = ((kpos >= col_start) & (kpos < col_start + CB)).astype(jnp.float32)
+
+    @pl.when(me == 0)
+    def _():
+        prev[...] = jnp.zeros_like(prev)
+
+    @pl.when(me == n - 1)
+    def _():
+        back[...] = jnp.zeros_like(back)
+
+    @pl.when(has_other)
+    def _():
+        pl.semaphore_wait(barrier, S + len(dsteps) + 1)
+
+    @pl.when((other < 0) | (other >= n))
+    def _():
+        pl.semaphore_wait(barrier, S + len(dsteps))
+
+    def gather_step(s):
+        return pltpu.make_async_remote_copy(
+            src_ref=col,
+            dst_ref=colr.at[s],
+            send_sem=cg_s.at[s],
+            recv_sem=cg_r.at[s],
+            device_id={"ctx": flip(me, steps[s])},
+            device_id_type=MESH,
+        )
+
+    def halo(i, h):
+        c = pl.ds(pl.multiple_of(h * D, D), D)
+        return pltpu.make_async_remote_copy(
+            src_ref=(k_ref, v_ref)[i].at[:, c],
+            dst_ref=prev.at[i, :, c],
+            send_sem=halo_s.at[i, h],
+            recv_sem=halo_r.at[i, h],
+            device_id={"ctx": me + 1},
+            device_id_type=MESH,
+        )
+
+    def give_back(i, h):
+        c = pl.ds(pl.multiple_of(h * D, D), D)
+        return pltpu.make_async_remote_copy(
+            src_ref=out.at[i, :, c],
+            dst_ref=back.at[i, :, c],
+            send_sem=ret_s.at[i, h],
+            recv_sem=ret_r.at[i, h],
+            device_id={"ctx": me - 1},
+            device_id_type=MESH,
+        )
+
+    def reduce_step(s, h):
+        return pltpu.make_async_remote_copy(
+            src_ref=acc.at[h],
+            dst_ref=accr.at[s, h],
+            send_sem=red_s.at[s, h],
+            recv_sem=red_r.at[s, h],
+            device_id={"ctx": flip(me, steps[s])},
+            device_id_type=MESH,
+        )
+
+    def send_halo():
+        @pl.when(me < n - 1)
+        def _():
+            @pl.loop(0, HEADS)
+            def _(h):
+                halo(0, h).start()
+                halo(1, h).start()
+
+    for s in range(S):
+        gather_step(s).start()
+        if s == S - 1:
+            send_halo()
+        gather_step(s).wait()
+        col[...] = col[...] + colr[s]
+
+    def compute(h):
+        @pl.when(me > 0)
+        def _():
+            halo(0, h).wait_recv()
+            halo(1, h).wait_recv()
+
+        c = pl.ds(pl.multiple_of(h * D, D), D)
+        bias2 = bias_ref[pl.ds(h, 1), :] * LOG2E
+        outside = jnp.where(me == 0, NEG, 0.0)
+        kc = col[0:CB, c]
+        vc = col[CB : 2 * CB, c]
+        keys = [prev[0, 0:HALF, c], prev[0, HALF:T, c], k_ref[0:HALF, c], k_ref[HALF:T, c]]
+        vals = [prev[1, 0:HALF, c], prev[1, HALF:T, c], v_ref[0:HALF, c], v_ref[HALF:T, c]]
+        dks = [None] * 4
+        dvs = [None] * 4
+        dkc = dvc = None
+        dbv = jnp.zeros((1, 128), jnp.float32)
+        for b in range(2):
+            rows = slice(b * HALF, (b + 1) * HALF)
+            qb = q_ref[rows, c]
+            gb = g_ref[rows, c]
+            scores = []
+            for p in range(3):
+                j = b + p
+                kb = flag[j * HALF : (j + 1) * HALF, :] * bias2
+                if j < 2:
+                    kb = kb + outside
+                s = dot_nt(keys[j], qb) * (SCALE * LOG2E) + jnp.concatenate([kb, kb], axis=1)
+                if p == 0:
+                    s = s + masks[0]
+                if p == 2:
+                    s = s + masks[1]
+                scores.append(s)
+            cpos = col_start2 + lax.broadcasted_iota(jnp.int32, (CB, HALF), 0)
+            qpos = start + b * HALF + lax.broadcasted_iota(jnp.int32, (CB, HALF), 1)
+            sc = dot_nt(kc, qb) * (SCALE * LOG2E) + jnp.concatenate([bias2, bias2], axis=1)
+            scores.append(jnp.where(cpos <= qpos - LOCAL_BAND, sc, NEG))
+            top = functools.reduce(
+                jnp.maximum, [jnp.max(s, axis=0, keepdims=True) for s in scores]
+            )
+            ps = [jnp.exp2(s - top) for s in scores]
+            total = functools.reduce(jnp.add, [jnp.sum(p, axis=0, keepdims=True) for p in ps])
+            inv = 1.0 / total
+            ws = [p * inv for p in ps]
+            w16 = [w.astype(jnp.bfloat16) for w in ws]
+            vb = [vals[b], vals[b + 1], vals[b + 2], vc]
+            kb = [keys[b], keys[b + 1], keys[b + 2], kc]
+            ot = functools.reduce(jnp.add, [dot_tn(v, w) for v, w in zip(vb, w16)])
+            ot = ot.astype(jnp.bfloat16).astype(jnp.float32)
+            o_ref[rows, c] = ot.T.astype(jnp.bfloat16)
+            delta = jnp.sum(gb.astype(jnp.float32).T * ot, axis=0, keepdims=True)
+            ds = [w * (dot_nt(v, gb) - delta) for v, w in zip(vb, ws)]
+            for p in range(3):
+                j = b + p
+                f = flag[j * HALF : (j + 1) * HALF, :]
+                dbv = dbv + jnp.sum(fold(ds[p]) * f, axis=0, keepdims=True)
+            dbv = dbv + jnp.sum(fold(ds[3]), axis=0, keepdims=True)
+            ds16 = [d.astype(jnp.bfloat16) for d in ds]
+            dqt = functools.reduce(jnp.add, [dot_tn(k, d) for k, d in zip(kb, ds16)])
+            dq_ref[rows, c] = (dqt * SCALE).T.astype(jnp.bfloat16)
+            for p in range(3):
+                j = b + p
+                dv = dot_nn(w16[p], gb)
+                dk = dot_nn(ds16[p], qb)
+                dvs[j] = dv if dvs[j] is None else dvs[j] + dv
+                dks[j] = dk if dks[j] is None else dks[j] + dk
+            dv = dot_nn(w16[3], gb)
+            dk = dot_nn(ds16[3], qb)
+            dvc = dv if dvc is None else dvc + dv
+            dkc = dk if dkc is None else dkc + dk
+        for j in range(2):
+            rows = slice(j * HALF, (j + 1) * HALF)
+            out[0, rows, c] = (dks[j] * SCALE).astype(jnp.bfloat16)
+            out[1, rows, c] = dvs[j].astype(jnp.bfloat16)
+            own[0, rows, c] = dks[j + 2] * SCALE
+            own[1, rows, c] = dvs[j + 2]
+        acc[h, 0:CB, :] = dkc * SCALE
+        acc[h, CB : 2 * CB, :] = dvc
+        acc[h, 2 * CB :, :] = jnp.broadcast_to(dbv, (8, 128))
+
+        @pl.when(me > 0)
+        def _():
+            give_back(0, h).start()
+            give_back(1, h).start()
+
+    def finish(h):
+        @pl.when(me < n - 1)
+        def _():
+            give_back(0, h).wait_recv()
+            give_back(1, h).wait_recv()
+
+        c = pl.ds(pl.multiple_of(h * D, D), D)
+        for i, ref in ((0, dk_ref), (1, dv_ref)):
+            summed = acc[h, i * CB : (i + 1) * CB, :]
+            for r in range(T // CB):
+                rows = slice(r * CB, (r + 1) * CB)
+                held = (col_start == start + r * CB).astype(jnp.float32)
+                grad = own[i, rows, c] + back[i, rows, c].astype(jnp.float32) + summed * held
+                ref[rows, c] = grad.astype(jnp.bfloat16)
+
+    def turn(t, carry):
+        @pl.when(t < HEADS)
+        def _():
+            compute(t)
+
+        for s in range(S + 1):
+            h = t - s
+
+            @pl.when((h >= 0) & (h < HEADS))
+            def _():
+                if s > 0:
+                    reduce_step(s - 1, h).wait()
+                    acc[h] = acc[h] + accr[s - 1, h]
+                if s < S:
+                    reduce_step(s, h).start()
+                else:
+                    finish(h)
+
+        return carry
+
+    lax.fori_loop(0, HEADS + S, turn, 0)
+
+    for h in range(HEADS):
+        bacc[h : h + 1, :] = acc[h, 2 * CB : 2 * CB + 1, :]
+    for s in range(len(dsteps)):
+        copy = pltpu.make_async_remote_copy(
+            src_ref=bacc,
+            dst_ref=baccr.at[s],
+            send_sem=b_s.at[s],
+            recv_sem=b_r.at[s],
+            device_id={"dp": flip(mine, dsteps[s])},
+            device_id_type=MESH,
+        )
+        copy.start()
+        copy.wait()
+        bacc[...] = bacc[...] + baccr[s]
+    db_ref[...] = bacc[...]
+
+    @pl.when(me < n - 1)
+    def _():
+        @pl.loop(0, HEADS)
+        def _(h):
+            halo(0, h).wait_send()
+            halo(1, h).wait_send()
+
+    @pl.when(me > 0)
+    def _():
+        @pl.loop(0, HEADS)
+        def _(h):
+            give_back(0, h).wait_send()
+            give_back(1, h).wait_send()
+
+
+def per_device(queries, key_vectors, value_vectors, out_grad, column_bias, column_offsets):
+    if column_offsets.shape[0] > 1:
+        return per_device_many_windows(
+            queries, key_vectors, value_vectors, out_grad, column_bias, column_offsets
+        )
+    n = lax.axis_size("ctx")
+    ndp = lax.axis_size("dp")
+    S = n.bit_length() - 1
+    SD = ndp.bit_length() - 1
+    width = queries.shape[2]
+    vmem = pl.BlockSpec(memory_space=pltpu.VMEM)
+    wide = jax.ShapeDtypeStruct((T, width), jnp.bfloat16)
+    o, dq, dk, dv, db = pl.pallas_call(
+        functools.partial(fused_kernel, n, ndp),
+        out_shape=(wide, wide, wide, wide, jax.ShapeDtypeStruct((HEADS, 128), jnp.float32)),
+        in_specs=[vmem, vmem, vmem, vmem, vmem, vmem],
+        out_specs=(vmem, vmem, vmem, vmem, vmem),
+        scratch_shapes=[
+            pltpu.VMEM((2, T, width), jnp.bfloat16),
+            pltpu.VMEM((2, T, width), jnp.bfloat16),
+            pltpu.VMEM((2, T, width), jnp.bfloat16),
+            pltpu.VMEM((2, T, width), jnp.float32),
+            pltpu.VMEM((2 * CB, width), jnp.bfloat16),
+            pltpu.VMEM((S, 2 * CB, width), jnp.bfloat16),
+            pltpu.VMEM((HEADS, 2 * CB + 8, 128), jnp.float32),
+            pltpu.VMEM((S, HEADS, 2 * CB + 8, 128), jnp.float32),
+            pltpu.VMEM((HEADS, 128), jnp.float32),
+            pltpu.VMEM((SD, HEADS, 128), jnp.float32),
+            pltpu.VMEM((2 * T, 128), jnp.float32),
+            pltpu.VMEM((2, HALF, HALF), jnp.float32),
+            pltpu.SemaphoreType.DMA((2, HEADS)),
+            pltpu.SemaphoreType.DMA((2, HEADS)),
+            pltpu.SemaphoreType.DMA((2, HEADS)),
+            pltpu.SemaphoreType.DMA((2, HEADS)),
+            pltpu.SemaphoreType.DMA((S,)),
+            pltpu.SemaphoreType.DMA((S,)),
+            pltpu.SemaphoreType.DMA((S, HEADS)),
+            pltpu.SemaphoreType.DMA((S, HEADS)),
+            pltpu.SemaphoreType.DMA((SD,)),
+            pltpu.SemaphoreType.DMA((SD,)),
+        ],
+        compiler_params=pltpu.CompilerParams(
+            collective_id=0, has_side_effects=True, vmem_limit_bytes=56 * 2**20
+        ),
+    )(
+        jnp.broadcast_to(column_offsets[:, None] * CB, (8, width)),
+        jnp.broadcast_to(column_bias[:, None], (HEADS, 128)),
+        queries[0],
+        key_vectors[0],
+        value_vectors[0],
+        out_grad[0],
+    )
+    return o[None], dq[None], dk[None], dv[None], jnp.sum(db, axis=1)
+
+
 def solution(mesh):
     placed = (
         P("dp", "ctx", None),

time: 357 us -> 107 us (0.30)
  matrix products: 133 us -> 0 us
  Pallas kernels: 0 us -> 95.8 us
  blocking collectives: 79.4 us -> 0 us
  waiting for transfers between devices: 37.1 us -> 0 us
  other arithmetic: 32.7 us -> 0.62 us
  local copies, waits for them, and re-layouts: 36.4 us -> 9.12 us
  between operations: 14.7 us -> 1.31 us
  starting transfers between devices: 10.7 us -> 0 us
  loops' own time: 10 us -> 0 us
    dot_general x96 -> x0, matrix products: 133 us -> none  [the longest x8 19.7 us: head_block(): jnp.dot(doh, vb.T, preferred_element_type=jnp.float32) - delta[:, None]]
    pallas_call x0 -> x1, Pallas kernels: none -> 95.8 us  [per_device(): pl.pallas_call(functools.partial(fused_kernel, n, ndp), out_shape=(wide,...]
    psum x1 -> x0, blocking collectives: 79.4 us -> none  [per_device(): bias_grad = lax.psum(dbias, ('dp', 'ctx'))]
    all_gather x2 -> x0, waiting for transfers between devices: 32.8 us -> none  [the longest x1 25.5 us: per_device(): lax.all_gather(piece_k, 'ctx', axis=0, tiled=True)]
    ppermute x4 -> x0, starting transfers between devices: 10.6 us -> none  [from_behind(): return lax.ppermute(value, axis, pairs)]
    select_n x9 -> x0, other arithmetic: 10.5 us -> none  [the longest x8 10.5 us: head_block(): jnp.where(band_col, bias_h, 0.0)[None, :]]
    another operation x1 -> x0, loops' own time: 10 us -> none  [per_device(): lax.map(per_head, (separate_heads(query_rows), separate_heads(band_k), se...]
    dynamic_slice x10 -> x0, local copies, waits for them, and re-layouts: 7.84 us -> none  [the longest x8 4.66 us: per_device(): lax.map(per_head, (separate_heads(query_rows), separate_heads(band_k), se...]
  transfers between devices with their start and end apart: 7 -> 0, of which waited for: 3 -> 0; matrix products, arithmetic and copies ran while one was open for 8% -> 0% of each run, Pallas kernels for 0% -> 0%
where the time goes in v1:
time: 107 us
  Pallas kernels  95.8 us (90%)
  local copies, waits for them, and re-layouts  9.12 us (9%)
  between operations  1.31 us (1%)
    pallas_call x1, Pallas kernels, per_device(): pl.pallas_call(functools.partial(fused_kernel, n, ndp), out_shape=(wide,...  95.8 us
    unnamed x14, local copies, waits for them, and re-layouts  7.84 us

profile of v1, /device:TPU:0, one launch (start us, length us, event | category | flops | bytes accessed | tf_op | source)
XLA Modules:
  0.0 106.9 jit_solution(7132531248235782342)
XLA Ops:
  1.3 0.0 copy-start.4
  1.3 0.6 copy-done.4
  1.9 0.7 broadcast_in_dim.28.bias_ref
  2.6 0.6 broadcast_in_dim.27.offs_ref
  3.2 95.8 %shard_map.101 = (bf16[512,1024]{1,0:T(8,128)(2,1)}, bf16[512,1024]{1,0:T(8,128)(2,1)}, bf16[512,1024]{1,0:T(8,128)(2,1)}, bf16[512,1024]{1,0:T(8,128)(2,1)}, f32[8,128]{1,0:T(8,128)}) custom-call(s32[8,1024]{1,0:T(8,128)} %broadcast_in_dim.27.offs_ref, f32[8,128]{1,0:T(8,128)} %broadcast_in_dim.28.bias_ref, bf16[512,1024]{1,0:T(8,128)(2,1)} %bitcast.9, ...), custom_call_target="tpu_custom_call" | custom-call | tf_op jit(solution)/shard_map/pallas_call | solution.py:512
  99.1 0.0 copy-start.3
  99.1 0.7 copy-done.3
  99.7 0.6 reduce_sum.9
  100.4 0.0 copy-start.2
  100.4 2.4 %copy.16 = bf16[1,512,1024]{2,1,0:T(8,128)(2,1)} copy(bf16[1,512,1024]{2,1,0:T(8,128)(2,1)} %bitcast.16) | data formatting | bytes 2097152
  102.7 0.0 copy-done.2
  102.7 0.0 copy-start.1
  102.7 1.0 copy.17
  103.7 0.6 copy-done.1
  104.3 0.0 copy-start
  104.3 1.0 copy.18
  105.3 0.6 copy-done
  105.9 1.0 copy.19
Async XLA Ops:
  1.3 0.7 copy-start.4
  99.1 0.7 copy-start.3
  100.4 2.4 %copy-start.2 = (bf16[512,1024]{1,0:T(8,128)(2,1)S(1)}, bf16[512,1024]{1,0:T(8,128)(2,1)}, u32[]{:S(2)}) copy-start(bf16[512,1024]{1,0:T(8,128)(2,1)} %get-tuple-element.11) | copy-start | bytes 3145732
  102.7 1.6 %copy-start.1 = (bf16[512,1024]{1,0:T(8,128)(2,1)S(1)}, bf16[512,1024]{1,0:T(8,128)(2,1)}, u32[]{:S(2)}) copy-start(bf16[512,1024]{1,0:T(8,128)(2,1)} %get-tuple-element.12) | copy-start | bytes 3145732
  104.3 1.6 %copy-start = (bf16[512,1024]{1,0:T(8,128)(2,1)S(1)}, bf16[512,1024]{1,0:T(8,128)(2,1)}, u32[]{:S(2)}) copy-start(bf16[512,1024]{1,0:T(8,128)(2,1)} %get-tuple-element.13) | copy-start | bytes 3145732

commit v2 on v1

--- a/solution.py
+++ b/solution.py
@@ -220,6 +220,9 @@
     baccr,
     flag,
     masks,
+    relay,
+    rel_s,
+    rel_r,
     halo_s,
     halo_r,
     ret_s,
@@ -245,8 +248,13 @@
     col_start = col_row[:, 0:128]
     col_start2 = col_row[:, 0:HALF]
 
+    even = me % 2 == 0
+    mid = n // 2
+    relayed = n == 8
     other = me + 2 * (me % 2) - 1
     has_other = (other >= 0) & (other < n)
+    ends = (me == 0) | (me == n - 1)
+    middle = (me == mid - 1) | (me == mid)
     barrier = pltpu.get_barrier_semaphore()
     for st in steps:
         pl.semaphore_signal(barrier, inc=1, device_id={"ctx": flip(me, st)}, device_id_type=MESH)
@@ -256,6 +264,12 @@
     @pl.when(has_other)
     def _():
         pl.semaphore_signal(barrier, inc=1, device_id={"ctx": other}, device_id_type=MESH)
+
+    if relayed:
+
+        @pl.when(ends | middle)
+        def _():
+            pl.semaphore_signal(barrier, inc=1, device_id={"ctx": flip(flip(me, 1), 2)}, device_id_type=MESH)
 
     for i, ref in ((0, k_ref), (1, v_ref)):
         block = jnp.zeros((CB, ref.shape[1]), jnp.float32)
@@ -279,13 +293,26 @@
     def _():
         back[...] = jnp.zeros_like(back)
 
-    @pl.when(has_other)
-    def _():
-        pl.semaphore_wait(barrier, S + len(dsteps) + 1)
-
-    @pl.when((other < 0) | (other >= n))
-    def _():
-        pl.semaphore_wait(barrier, S + len(dsteps))
+    peers = S + len(dsteps)
+    if relayed:
+
+        @pl.when(middle)
+        def _():
+            pl.semaphore_wait(barrier, peers + 2)
+
+        @pl.when((me != mid) & (me != mid - 1))
+        def _():
+            pl.semaphore_wait(barrier, peers + 1)
+
+    else:
+
+        @pl.when(has_other)
+        def _():
+            pl.semaphore_wait(barrier, peers + 1)
+
+        @pl.when(ends)
+        def _():
+            pl.semaphore_wait(barrier, peers)
 
     def gather_step(s):
         return pltpu.make_async_remote_copy(
@@ -293,7 +320,7 @@
             dst_ref=colr.at[s],
             send_sem=cg_s.at[s],
             recv_sem=cg_r.at[s],
-            device_id={"ctx": flip(me, steps[s])},
+            device_id={"ctx": flip(me, (steps + [1])[s])},
             device_id_type=MESH,
         )
 
@@ -325,24 +352,68 @@
             dst_ref=accr.at[s, h],
             send_sem=red_s.at[s, h],
             recv_sem=red_r.at[s, h],
-            device_id={"ctx": flip(me, steps[s])},
+            device_id={"ctx": flip(me, (steps + [1])[s])},
             device_id_type=MESH,
         )
 
+    def hop(i, h, first, source, target, to, send, recv):
+        c = pl.ds(pl.multiple_of(h * D, D), D)
+        return pltpu.make_async_remote_copy(
+            src_ref=source.at[:, c] if first else source.at[i, :, c],
+            dst_ref=target.at[i, :, c],
+            send_sem=send.at[i, h],
+            recv_sem=recv.at[i, h],
+            device_id={"ctx": to},
+            device_id_type=MESH,
+        )
+
+    def halo_out(i, h):
+        return hop(i, h, True, (k_ref, v_ref)[i], relay, n - 1, halo_s, rel_r)
+
+    def halo_on(i, h):
+        return hop(i, h, False, relay, prev, mid, rel_s, halo_r)
+
+    def back_out(i, h):
+        return hop(i, h, False, out, relay, 0, ret_s, rel_r)
+
+    def back_on(i, h):
+        return hop(i, h, False, relay, back, mid - 1, rel_s, ret_r)
+
     def send_halo():
+        round_about = (me == mid - 1) if relayed else (me < 0)
+
         @pl.when(me < n - 1)
         def _():
             @pl.loop(0, HEADS)
             def _(h):
-                halo(0, h).start()
-                halo(1, h).start()
-
-    for s in range(S):
-        gather_step(s).start()
-        if s == S - 1:
-            send_halo()
-        gather_step(s).wait()
-        col[...] = col[...] + colr[s]
+                @pl.when(round_about & (h % 2 == 1))
+                def _():
+                    halo_out(0, h).start()
+                    halo_out(1, h).start()
+
+                @pl.when((me != mid - 1) | (h % 2 == 0) if relayed else (me >= 0))
+                def _():
+                    halo(0, h).start()
+                    halo(1, h).start()
+
+    send_halo()
+
+    @pl.when(me % 2 == 1)
+    def _():
+        gather_step(0).start()
+        gather_step(0).wait_send()
+        gather_step(S).wait_recv()
+        col[...] = colr[S]
+
+    @pl.when(even)
+    def _():
+        gather_step(0).wait_recv()
+        col[...] = col[...] + colr[0]
+        for s in range(1, S):
+            gather_step(s).start()
+            gather_step(s).wait()
+            col[...] = col[...] + colr[s]
+        gather_step(S).start()
 
     def compute(h):
         @pl.when(me > 0)
@@ -424,7 +495,14 @@
         acc[h, CB : 2 * CB, :] = dvc
         acc[h, 2 * CB :, :] = jnp.broadcast_to(dbv, (8, 128))
 
-        @pl.when(me > 0)
+        if relayed:
+
+            @pl.when((me == mid) & (h % 2 == 0))
+            def _():
+                back_out(0, h).start()
+                back_out(1, h).start()
+
+        @pl.when((me > 0) & ((me != mid) | (h % 2 == 1)) if relayed else (me > 0))
         def _():
             give_back(0, h).start()
             give_back(1, h).start()
@@ -449,22 +527,52 @@
         def _():
             compute(t)
 
-        for s in range(S + 1):
+        @pl.when(even & (t < HEADS))
+        def _():
+            reduce_step(0, t).start()
+
+        for s in range(1, S + 1):
             h = t - s
 
-            @pl.when((h >= 0) & (h < HEADS))
+            @pl.when((me % 2 == 1) & (h >= 0) & (h < HEADS))
             def _():
-                if s > 0:
+                if s == 1:
+                    reduce_step(0, h).wait_recv()
+                else:
                     reduce_step(s - 1, h).wait()
-                    acc[h] = acc[h] + accr[s - 1, h]
-                if s < S:
-                    reduce_step(s, h).start()
-                else:
+                acc[h] = acc[h] + accr[s - 1, h]
+                reduce_step(s, h).start()
+                if s == S:
                     finish(h)
 
+        last = t - S - 1
+
+        @pl.when(even & (last >= 0))
+        def _():
+            reduce_step(0, last).wait_send()
+            reduce_step(S, last).wait_recv()
+            acc[last] = accr[S, last]
+            finish(last)
+
+        if relayed:
+
+            @pl.when((me == n - 1) & (t < HEADS // 2))
+            def _():
+                h = 2 * t + 1
+                for i in range(2):
+                    halo_out(i, h).wait_recv()
+                    halo_on(i, h).start()
+
+            @pl.when((me == 0) & (t >= 1) & (t <= HEADS) & (t % 2 == 1))
+            def _():
+                h = t - 1
+                for i in range(2):
+                    back_out(i, h).wait_recv()
+                    back_on(i, h).start()
+
         return carry
 
-    lax.fori_loop(0, HEADS + S, turn, 0)
+    lax.fori_loop(0, HEADS + S + 1, turn, 0)
 
     for h in range(HEADS):
         bacc[h : h + 1, :] = acc[h, 2 * CB : 2 * CB + 1, :]
@@ -481,6 +589,25 @@
         copy.wait()
         bacc[...] = bacc[...] + baccr[s]
     db_ref[...] = bacc[...]
+
+    @pl.when(even)
+    def _():
+        gather_step(S).wait_send()
+
+    @pl.when(me % 2 == 1)
+    def _():
+        @pl.loop(0, HEADS)
+        def _(h):
+            reduce_step(S, h).wait_send()
+
+    if relayed:
+
+        @pl.when(ends)
+        def _():
+            @pl.loop(0, HEADS // 2)
+            def _(g):
+                for i in range(2):
+                    halo_on(i, 2 * g + me % 2).wait_send()
 
     @pl.when(me < n - 1)
     def _():
@@ -520,21 +647,24 @@
             pltpu.VMEM((2, T, width), jnp.bfloat16),
             pltpu.VMEM((2, T, width), jnp.float32),
             pltpu.VMEM((2 * CB, width), jnp.bfloat16),
-            pltpu.VMEM((S, 2 * CB, width), jnp.bfloat16),
+            pltpu.VMEM((S + 1, 2 * CB, width), jnp.bfloat16),
             pltpu.VMEM((HEADS, 2 * CB + 8, 128), jnp.float32),
-            pltpu.VMEM((S, HEADS, 2 * CB + 8, 128), jnp.float32),
+            pltpu.VMEM((S + 1, HEADS, 2 * CB + 8, 128), jnp.float32),
             pltpu.VMEM((HEADS, 128), jnp.float32),
             pltpu.VMEM((SD, HEADS, 128), jnp.float32),
             pltpu.VMEM((2 * T, 128), jnp.float32),
             pltpu.VMEM((2, HALF, HALF), jnp.float32),
+            pltpu.VMEM((2, T, width), jnp.bfloat16),
             pltpu.SemaphoreType.DMA((2, HEADS)),
             pltpu.SemaphoreType.DMA((2, HEADS)),
             pltpu.SemaphoreType.DMA((2, HEADS)),
             pltpu.SemaphoreType.DMA((2, HEADS)),
-            pltpu.SemaphoreType.DMA((S,)),
-            pltpu.SemaphoreType.DMA((S,)),
-            pltpu.SemaphoreType.DMA((S, HEADS)),
-            pltpu.SemaphoreType.DMA((S, HEADS)),
+            pltpu.SemaphoreType.DMA((2, HEADS)),
+            pltpu.SemaphoreType.DMA((2, HEADS)),
+            pltpu.SemaphoreType.DMA((S + 1,)),
+            pltpu.SemaphoreType.DMA((S + 1,)),
+            pltpu.SemaphoreType.DMA((S + 1, HEADS)),
+            pltpu.SemaphoreType.DMA((S + 1, HEADS)),
             pltpu.SemaphoreType.DMA((SD,)),
             pltpu.SemaphoreType.DMA((SD,)),
         ],

time: 107 us -> 90.8 us (0.85)
  Pallas kernels: 95.8 us -> 79.5 us
    pallas_call x1, Pallas kernels: 95.8 us -> 79.5 us  [per_device(): pl.pallas_call(functools.partial(fused_kernel, n, ndp), out_shape=(wide,...]
where the time goes in v2:
time: 90.8 us; the launch traced here: 90.5 us
  Pallas kernels  79.5 us (88%)
  local copies, waits for them, and re-layouts  9.12 us (10%)
  between operations  1.31 us (1%)
    pallas_call x1, Pallas kernels, per_device(): pl.pallas_call(functools.partial(fused_kernel, n, ndp), out_shape=(wide,...  79.5 us
    unnamed x14, local copies, waits for them, and re-layouts  7.84 us

profile of v2, /device:TPU:0, one launch (start us, length us, event | category | flops | bytes accessed | tf_op | source)
XLA Modules:
  0.0 90.5 jit_solution(15111746044054795915)
XLA Ops:
  1.3 0.0 copy-start.4
  1.3 0.6 copy-done.4
  1.9 0.7 broadcast_in_dim.28.bias_ref
  2.6 0.6 broadcast_in_dim.27.offs_ref
  3.2 79.5 %shard_map.101 = (bf16[512,1024]{1,0:T(8,128)(2,1)}, bf16[512,1024]{1,0:T(8,128)(2,1)}, bf16[512,1024]{1,0:T(8,128)(2,1)}, bf16[512,1024]{1,0:T(8,128)(2,1)}, f32[8,128]{1,0:T(8,128)}) custom-call(s32[8,1024]{1,0:T(8,128)} %broadcast_in_dim.27.offs_ref, f32[8,128]{1,0:T(8,128)} %broadcast_in_dim.28.bias_ref, bf16[512,1024]{1,0:T(8,128)(2,1)} %bitcast.9, ...), custom_call_target="tpu_custom_call" | custom-call | tf_op jit(solution)/shard_map/pallas_call | solution.py:639
  82.7 0.0 copy-start.3
  82.7 0.7 copy-done.3
  83.4 0.6 reduce_sum.9
  84.0 0.0 copy-start.2
  84.0 2.4 %copy.16 = bf16[1,512,1024]{2,1,0:T(8,128)(2,1)} copy(bf16[1,512,1024]{2,1,0:T(8,128)(2,1)} %bitcast.16) | data formatting | bytes 2097152
  86.4 0.0 copy-done.2
  86.4 0.0 copy-start.1
  86.4 1.0 %copy.17 = bf16[1,512,1024]{2,1,0:T(8,128)(2,1)} copy(bf16[1,512,1024]{2,1,0:T(8,128)(2,1)S(1)} %bitcast.15) | data formatting | bytes 2097152
  87.3 0.6 copy-done.1
  88.0 0.0 copy-start
  88.0 1.0 %copy.18 = bf16[1,512,1024]{2,1,0:T(8,128)(2,1)} copy(bf16[1,512,1024]{2,1,0:T(8,128)(2,1)S(1)} %bitcast.14) | data formatting | bytes 2097152
  88.9 0.6 copy-done
  89.6 1.0 %copy.19 = bf16[1,512,1024]{2,1,0:T(8,128)(2,1)} copy(bf16[1,512,1024]{2,1,0:T(8,128)(2,1)S(1)} %bitcast.13) | data formatting | bytes 2097152
Async XLA Ops:
  1.3 0.7 copy-start.4
  82.7 0.7 copy-start.3
  84.0 2.4 %copy-start.2 = (bf16[512,1024]{1,0:T(8,128)(2,1)S(1)}, bf16[512,1024]{1,0:T(8,128)(2,1)}, u32[]{:S(2)}) copy-start(bf16[512,1024]{1,0:T(8,128)(2,1)} %get-tuple-element.11) | copy-start | bytes 3145732
  86.4 1.6 %copy-start.1 = (bf16[512,1024]{1,0:T(8,128)(2,1)S(1)}, bf16[512,1024]{1,0:T(8,128)(2,1)}, u32[]{:S(2)}) copy-start(bf16[512,1024]{1,0:T(8,128)(2,1)} %get-tuple-element.12) | copy-start | bytes 3145732
  88.0 1.6 %copy-start = (bf16[512,1024]{1,0:T(8,128)(2,1)S(1)}, bf16[512,1024]{1,0:T(8,128)(2,1)}, u32[]{:S(2)}) copy-start(bf16[512,1024]{1,0:T(8,128)(2,1)} %get-tuple-element.13) | copy-start | bytes 3145732

commit v3 on v2

--- a/solution.py
+++ b/solution.py
@@ -250,7 +250,7 @@
 
     even = me % 2 == 0
     mid = n // 2
-    relayed = n == 8
+    relayed = False
     other = me + 2 * (me % 2) - 1
     has_other = (other >= 0) & (other < n)
     ends = (me == 0) | (me == n - 1)

time: 90.8 us -> 88.2 us (0.971); the launches traced: 90.5 us -> 86.9 us
  Pallas kernels: 79.5 us -> 75.9 us
    pallas_call x1, Pallas kernels: 79.5 us -> 75.9 us  [per_device(): pl.pallas_call(functools.partial(fused_kernel, n, ndp), out_shape=(wide,...]
where the time goes in v3:
time: 88.2 us; the launch traced here: 86.9 us
  Pallas kernels  75.9 us (86%)
  local copies, waits for them, and re-layouts  9.12 us (10%)
  between operations  1.31 us (1%)
    pallas_call x1, Pallas kernels, per_device(): pl.pallas_call(functools.partial(fused_kernel, n, ndp), out_shape=(wide,...  75.9 us
    unnamed x14, local copies, waits for them, and re-layouts  7.84 us

profile of v3, /device:TPU:0, one launch (start us, length us, event | category | flops | bytes accessed | tf_op | source)
XLA Modules:
  0.0 86.9 jit_solution(5964974389114425840)
XLA Ops:
  1.3 0.0 copy-start.4
  1.3 0.6 copy-done.4
  1.9 0.7 broadcast_in_dim.28.bias_ref
  2.6 0.6 broadcast_in_dim.27.offs_ref
  3.2 75.9 %shard_map.101 = (bf16[512,1024]{1,0:T(8,128)(2,1)}, bf16[512,1024]{1,0:T(8,128)(2,1)}, bf16[512,1024]{1,0:T(8,128)(2,1)}, bf16[512,1024]{1,0:T(8,128)(2,1)}, f32[8,128]{1,0:T(8,128)}) custom-call(s32[8,1024]{1,0:T(8,128)} %broadcast_in_dim.27.offs_ref, f32[8,128]{1,0:T(8,128)} %broadcast_in_dim.28.bias_ref, bf16[512,1024]{1,0:T(8,128)(2,1)} %bitcast.9, ...), custom_call_target="tpu_custom_call" | custom-call | tf_op jit(solution)/shard_map/pallas_call | solution.py:639
  79.1 0.0 copy-start.3
  79.1 0.7 copy-done.3
  79.8 0.6 reduce_sum.9
  80.4 0.0 copy-start.2
  80.4 2.4 %copy.16 = bf16[1,512,1024]{2,1,0:T(8,128)(2,1)} copy(bf16[1,512,1024]{2,1,0:T(8,128)(2,1)} %bitcast.16) | data formatting | bytes 2097152
  82.7 0.0 copy-done.2
  82.7 0.0 copy-start.1
  82.7 1.0 %copy.17 = bf16[1,512,1024]{2,1,0:T(8,128)(2,1)} copy(bf16[1,512,1024]{2,1,0:T(8,128)(2,1)S(1)} %bitcast.15) | data formatting | bytes 2097152
  83.7 0.6 copy-done.1
  84.3 0.0 copy-start
  84.3 1.0 %copy.18 = bf16[1,512,1024]{2,1,0:T(8,128)(2,1)} copy(bf16[1,512,1024]{2,1,0:T(8,128)(2,1)S(1)} %bitcast.14) | data formatting | bytes 2097152
  85.3 0.6 copy-done
  85.9 1.0 %copy.19 = bf16[1,512,1024]{2,1,0:T(8,128)(2,1)} copy(bf16[1,512,1024]{2,1,0:T(8,128)(2,1)S(1)} %bitcast.13) | data formatting | bytes 2097152
Async XLA Ops:
  1.3 0.7 copy-start.4
  79.1 0.7 copy-start.3
  80.4 2.4 %copy-start.2 = (bf16[512,1024]{1,0:T(8,128)(2,1)S(1)}, bf16[512,1024]{1,0:T(8,128)(2,1)}, u32[]{:S(2)}) copy-start(bf16[512,1024]{1,0:T(8,128)(2,1)} %get-tuple-element.11) | copy-start | bytes 3145732
  82.7 1.6 %copy-start.1 = (bf16[512,1024]{1,0:T(8,128)(2,1)S(1)}, bf16[512,1024]{1,0:T(8,128)(2,1)}, u32[]{:S(2)}) copy-start(bf16[512,1024]{1,0:T(8,128)(2,1)} %get-tuple-element.12) | copy-start | bytes 3145732
  84.3 1.6 %copy-start = (bf16[512,1024]{1,0:T(8,128)(2,1)S(1)}, bf16[512,1024]{1,0:T(8,128)(2,1)}, u32[]{:S(2)}) copy-start(bf16[512,1024]{1,0:T(8,128)(2,1)} %get-tuple-element.13) | copy-start | bytes 3145732
